TPU v7x, 32 devices: a whole 2x2x4 slice. The times are simulated.
32 devices in a mesh: ctx: 8 (over z, x), head: 4 (over y, core).
Axes of the slice: x: 2, y: 2, z: 4, core: 2. Of those that a mesh axis runs over, the one named last changes fastest.
Arguments:
- token_keys: bfloat16 [8, 2048, 128], P(None, ('ctx', 'head')), may hold values from -4.5 to 4.5
- token_values: bfloat16 [8, 2048, 128], P(None, ('ctx', 'head')), may hold values from -6 to 6
- queries: bfloat16 [8, 2048, 8, 128], P(None, ('ctx', 'head')), may hold values from -16 to 16
- out_grad: bfloat16 [8, 2048, 8, 128], P(None, ('ctx', 'head')), may hold values from -6 to 6
- slot_ids: int32 [8, 2048], P('head'), may hold values from 0 to 511, as said below
Outputs:
- attended: bfloat16 [8, 2048, 8, 128], P(None, ('ctx', 'head'))
- key_grad: float32 [8, 2048, 128], P(None, ('ctx', 'head'))
- value_grad: float32 [8, 2048, 128], P(None, ('ctx', 'head'))
Inputs may be any that keep to these rules, and one draw needn't show every extreme that they name: `slot_ids`: in each head's row slot numbers never fall; each of the 512 slots holds 1 to 16 consecutive tokens; slots k * 64 to (k + 1) * 64 - 1 all begin among tokens k * 256 to (k + 1) * 256 - 1; every such block of tokens holds a slot of exactly 16 tokens.
All inputs are finite; a program needn't handle non-finite values.
Results may differ from a plain program's by a relative error of at most 0.012.
The roundings to bfloat16 on the way count: a program that leaves them out, or rounds other values in their place, can miss the bound.
Values may be sent and summed in bfloat16 or wider, within the bound.
A program may use at most 64 MiB of HBM per device.

v0:
```python
import math
import jax
import jax.numpy as jnp
from jax import lax
from jax.sharding import PartitionSpec as P

RATIO = 4
neg_big = -1e30


def from_behind(value, axis, steps):
    count = lax.axis_size(axis)
    initial, last = (max(0, -steps), min(count, count - steps))
    return lax.ppermute(value, axis, [(source, source + steps) for source in range(initial, last)])


def one_hot_rows(own_ids, first_row, how_many):
    relative = own_ids - first_row
    columns = jnp.arange(how_many, dtype=jnp.int32)
    return (relative[:, :, None] == columns[None, None, :]).astype(jnp.bfloat16)


def per_device(token_keys, token_values, queries, out_grad, slot_ids):
    keys_here, values_here, query_here, grad_here = (
        lax.all_to_all(token_keys, "head", split_axis=0, concat_axis=1, tiled=True),
        lax.all_to_all(token_values, "head", split_axis=0, concat_axis=1, tiled=True),
        lax.all_to_all(queries, "head", split_axis=0, concat_axis=1, tiled=True),
        lax.all_to_all(out_grad, "head", split_axis=0, concat_axis=1, tiled=True),
    )
    local_heads, tok_count, head_dim = keys_here.shape
    query_count = query_here.shape[1]
    group_size = query_here.shape[2]
    slot_count = tok_count // RATIO
    id_heads, context_len = slot_ids.shape
    total_slots = context_len // RATIO
    block_count = context_len // tok_count
    ctx_index = lax.axis_index("ctx")
    blocked_ids = slot_ids.reshape(id_heads, block_count, tok_count)
    block_base = jnp.arange(block_count, dtype=jnp.int32)
    targets = block_base[:, None] * slot_count + jnp.arange(slot_count, dtype=jnp.int32)[None, :]
    below_count = jnp.sum(
        (blocked_ids[:, :, :, None] < targets[None, :, None, :]).astype(jnp.int32), axis=2
    )
    starts_all = (block_base[None, :, None] * tok_count + below_count).reshape(
        id_heads, total_slots
    )
    slot_edges = jnp.concatenate(
        [starts_all, jnp.full((id_heads, 1), context_len, jnp.int32)], axis=1
    )
    slot_start = starts_all.T
    slot_len = slot_edges[:, 1:] - slot_edges[:, :-1]
    lengths_t = slot_len.T.astype(jnp.float32)[:, :, None]
    own_ids = lax.dynamic_slice_in_dim(slot_ids, ctx_index * tok_count, tok_count, 1)
    pair_low = jnp.concatenate([keys_here, values_here], axis=2)
    first_slot = ctx_index * slot_count - 1
    hot = one_hot_rows(own_ids, first_slot, slot_count + 1)
    window = jnp.einsum("htn,htc->nhc", hot, pair_low, preferred_element_type=jnp.float32)
    carried = from_behind(window[:1], "ctx", -1)
    padding = jnp.zeros((slot_count - 1, local_heads, 2 * head_dim), jnp.float32)
    own_sums = window[1:] + jnp.concatenate([padding, carried], axis=0)
    own_len = lax.dynamic_slice_in_dim(lengths_t, ctx_index * slot_count, slot_count, 0)
    slot_pairs = (own_sums / own_len).astype(jnp.bfloat16)
    rows_here = query_count * group_size
    query_rows = query_here.reshape(local_heads, rows_here, head_dim)
    grad_rows = grad_here.reshape(local_heads, rows_here, head_dim)
    stride = tok_count // query_count
    positions = jnp.repeat(
        (ctx_index * query_count + jnp.arange(query_count, dtype=jnp.int32)) * stride + stride - 1,
        group_size,
    )
    last_position = (ctx_index + 1) * query_count * stride - 1
    score_scale = 1.0 / math.sqrt(head_dim)

    def block_scores(key_block):
        scores = (
            jnp.einsum("hrd,nhd->hrn", query_rows, key_block, preferred_element_type=jnp.float32)
            * score_scale
        )
        visible = slot_start.T[:, None, :] <= positions[None, :, None]
        return (scores, visible)

    def reaches(first_row):
        return (
            jnp.min(lax.dynamic_index_in_dim(slot_start, first_row, 0, keepdims=False))
            <= last_position
        )

    init_stats = (
        jnp.full((local_heads, rows_here), neg_big, jnp.float32),
        jnp.zeros((local_heads, rows_here), jnp.float32),
    )
    key_block = lax.all_gather(slot_pairs[:, :, :head_dim], "ctx", axis=0, tiled=True)

    def stats_advance(state_in):
        top_now, mass_now = state_in
        scores, visible = block_scores(key_block)
        top_new = jnp.maximum(top_now, jnp.max(jnp.where(visible, scores, neg_big), axis=2))
        fresh = jnp.sum(jnp.where(visible, jnp.exp(scores - top_new[:, :, None]), 0.0), axis=2)
        return (top_new, fresh)

    row_top, row_mass = lax.cond(
        reaches(jnp.int32(0)), stats_advance, lambda state_in: state_in, init_stats
    )
    log_total = row_top + jnp.log(row_mass)

    def weights_of(pair_block):
        scores, visible = block_scores(pair_block[:, :, :head_dim])
        return jnp.where(visible, jnp.exp(scores - log_total[:, :, None]), 0.0)

    init_acc = jnp.zeros((local_heads, rows_here, head_dim), jnp.float32)
    pair_block = lax.all_gather(slot_pairs, "ctx", axis=0, tiled=True)

    def value_advance(state_in):
        weights_low = weights_of(pair_block).astype(jnp.bfloat16)
        return jnp.einsum(
            "hrn,nhd->hrd",
            weights_low,
            pair_block[:, :, head_dim:],
            preferred_element_type=jnp.float32,
        )

    summed_out = lax.cond(reaches(jnp.int32(0)), value_advance, lambda state_in: state_in, init_acc)
    attended = summed_out.astype(jnp.bfloat16)
    out_back = lax.all_to_all(
        attended.reshape(local_heads, query_count, group_size, head_dim),
        "head",
        split_axis=1,
        concat_axis=0,
        tiled=True,
    )
    row_dot = jnp.sum(grad_rows.astype(jnp.float32) * attended.astype(jnp.float32), axis=2)
    init_partials = jnp.zeros((total_slots, local_heads, 2 * head_dim), jnp.float32)
    grad_pair_block = lax.all_gather(slot_pairs, "ctx", axis=0, tiled=True)

    def grad_advance(state_in):
        weights = weights_of(grad_pair_block)
        weights_low = weights.astype(jnp.bfloat16)
        value_grads = jnp.einsum(
            "hrn,hrd->nhd", weights_low, grad_rows, preferred_element_type=jnp.float32
        )
        weight_grads = jnp.einsum(
            "hrd,nhd->hrn",
            grad_rows,
            grad_pair_block[:, :, head_dim:],
            preferred_element_type=jnp.float32,
        )
        dscores = (weights * (weight_grads - row_dot[:, :, None])).astype(jnp.bfloat16)
        key_grads = (
            jnp.einsum("hrn,hrd->nhd", dscores, query_rows, preferred_element_type=jnp.float32)
            * score_scale
        )
        return jnp.concatenate([key_grads, value_grads], axis=2)

    partials = lax.cond(
        reaches(jnp.int32(0)), grad_advance, lambda state_in: state_in, init_partials
    )
    share_grads = lax.psum_scatter(
        partials.astype(jnp.bfloat16), "ctx", scatter_dimension=0, tiled=True
    )
    below_row = from_behind(share_grads[-1:], "ctx", 1)
    grad_window = jnp.concatenate([below_row, share_grads], axis=0)
    hot = one_hot_rows(own_ids, first_slot, grad_window.shape[0])
    token_sums = jnp.einsum("htn,nhc->htc", hot, grad_window, preferred_element_type=jnp.float32)
    padded_len = jnp.concatenate([jnp.ones((id_heads, 1), jnp.int32), slot_len], axis=1)
    window_len = lax.dynamic_slice_in_dim(padded_len, first_slot + 1, slot_count + 1, 1).astype(
        jnp.float32
    )
    relative_ids = own_ids - first_slot
    window_cols = jnp.arange(slot_count + 1, dtype=jnp.int32)
    token_len = jnp.sum(
        jnp.where(
            relative_ids[:, :, None] == window_cols[None, None, :], window_len[:, None, :], 0.0
        ),
        axis=2,
    )[:, :, None]
    token_grads = token_sums / token_len
    key_back, value_back = (
        lax.all_to_all(
            token_grads[:, :, :head_dim].astype(jnp.bfloat16),
            "head",
            split_axis=1,
            concat_axis=0,
            tiled=True,
        ).astype(jnp.float32),
        lax.all_to_all(
            token_grads[:, :, head_dim:].astype(jnp.bfloat16),
            "head",
            split_axis=1,
            concat_axis=0,
            tiled=True,
        ).astype(jnp.float32),
    )
    return (out_back, key_back, value_back)


def solution(mesh):
    placed = (
        P(None, ("ctx", "head"), None),
        P(None, ("ctx", "head"), None),
        P(None, ("ctx", "head"), None, None),
        P(None, ("ctx", "head"), None, None),
        P("head", None),
    )
    return jax.shard_map(
        per_device,
        mesh=mesh,
        in_specs=placed,
        out_specs=(
            P(None, ("ctx", "head"), None, None),
            P(None, ("ctx", "head"), None),
            P(None, ("ctx", "head"), None),
        ),
        check_vma=False,
    )
```

profile of v0, /device:TPU:8, one launch (start us, length us, event | category | flops | bytes accessed | tf_op | source)
XLA Modules:
  0.0 240.5 jit_solution(12412605172236448797)
XLA Ops:
  7.2 3.3 %all-to-all-start = ((bf16[8,64,128]{2,1,0:T(8,128)(2,1)}), bf16[8,64,128]{2,1,0:T(8,128)(2,1)S(1)}, u32[]{:S(2)}, u32[]{:S(2)}) async-start(bf16[8,64,128]{2,1,0:T(8,128)(2,1)} %param.11), calls=%async_computation | async-start | bytes 262144 | tf_op jit(solution)/shard_map/all_to_all | solution.py:25
  10.6 0.7 copy.73
  11.3 0.5 convert_reduce_fusion
  11.8 0.7 dynamic-slice_subtract_fusion
  12.5 2.6 %all-to-all-done = bf16[8,64,128]{2,1,0:T(8,128)(2,1)S(1)} async-done(((bf16[8,64,128]{2,1,0:T(8,128)(2,1)}), bf16[8,64,128]{2,1,0:T(8,128)(2,1)S(1)}, u32[]{:S(2)}, u32[]{:S(2)}) %all-to-all-start) | async-done | bytes 131104 | tf_op jit(solution)/shard_map/all_to_all | solution.py:25
  15.1 3.3 %all-to-all-start.1 = ((bf16[8,64,128]{2,1,0:T(8,128)(2,1)}), bf16[8,64,128]{2,1,0:T(8,128)(2,1)S(1)}, u32[]{:S(2)}, u32[]{:S(2)}) async-start(bf16[8,64,128]{2,1,0:T(8,128)(2,1)} %param.12), calls=%async_computation.1 | async-start | bytes 262144 | tf_op jit(solution)/shard_map/all_to_all | solution.py:26
  18.5 4.6 %all-to-all-done.1 = bf16[8,64,128]{2,1,0:T(8,128)(2,1)S(1)} async-done(((bf16[8,64,128]{2,1,0:T(8,128)(2,1)}), bf16[8,64,128]{2,1,0:T(8,128)(2,1)S(1)}, u32[]{:S(2)}, u32[]{:S(2)}) %all-to-all-start.1) | async-done | bytes 131104 | tf_op jit(solution)/shard_map/all_to_all | solution.py:26
  23.0 3.5 %all-to-all-start.2 = ((bf16[8,64,8,128]{3,2,1,0:T(8,128)(2,1)}), bf16[8,64,8,128]{3,2,1,0:T(8,128)(2,1)S(1)}, u32[]{:S(2)}, u32[]{:S(2)}) async-start(bf16[8,64,8,128]{3,2,1,0:T(8,128)(2,1)} %param.13), calls=%async_computation.2 | async-start | bytes 2097152 | tf_op jit(solution)/shard_map/all_to_all | solution.py:27
  26.8 0.6 slice_reduce_fusion
  27.6 13.4 %all-to-all-done.2 = bf16[8,64,8,128]{3,2,1,0:T(8,128)(2,1)S(1)} async-done(((bf16[8,64,8,128]{3,2,1,0:T(8,128)(2,1)}), bf16[8,64,8,128]{3,2,1,0:T(8,128)(2,1)S(1)}, u32[]{:S(2)}, u32[]{:S(2)}) %all-to-all-start.2) | async-done | bytes 1048608 | tf_op jit(solution)/shard_map/all_to_all | solution.py:27
  41.0 4.3 %all-to-all-start.4 = ((bf16[8,64,8,128]{3,2,1,0:T(8,128)(2,1)}), bf16[8,64,8,128]{3,2,1,0:T(8,128)(2,1)}, u32[]{:S(2)}, u32[]{:S(2)}) async-start(bf16[8,64,8,128]{3,2,1,0:T(8,128)(2,1)} %param.14), calls=%async_computation.4 | async-start | bytes 2097152 | tf_op jit(solution)/shard_map/all_to_all | solution.py:28
  45.3 0.2 convolution_bitcast_fusion
  45.5 3.3 %collective-permute-start = (f32[1,2,256]{2,0,1:T(1,128)S(1)}, f32[1,2,256]{2,0,1:T(1,128)S(1)}, u32[]{:S(2)}, u32[]{:S(2)}) collective-permute-start(f32[1,2,256]{2,0,1:T(1,128)S(1)} %slice.50), channel_id=1, source_target_pairs={{4,0},{8,4},{12,8},{16,12},{20,16},{24,20},{28,24},{5,1},{9,5},{13... | collective-permute-start | bytes 6152 | tf_op jit(solution)/shard_map/ppermute | solution.py:14
  49.5 1.5 collective-permute-done
  51.1 28.4 %all_gather.8 = bf16[512,2,128]{2,0,1:T(8,128)(2,1)S(1)} all-gather(bf16[64,2,128]{2,0,1:T(8,128)(2,1)S(1)} %slice.51), channel_id=1, replica_groups=mesh['ctx'=8,'head'=4] {'ctx'}, dimensions={0}, use_global_device_ids=true | all-gather | bytes 294912 | tf_op jit(solution)/shard_map/all_gather | solution.py:92
  79.5 31.5 %all_gather.7 = bf16[512,2,256]{2,0,1:T(8,128)(2,1)S(1)} all-gather(bf16[64,2,256]{2,0,1:T(8,128)(2,1)S(1)} %fusion.31), channel_id=1, replica_groups=mesh['ctx'=8,'head'=4] {'ctx'}, dimensions={0}, use_global_device_ids=true | all-gather | bytes 589824 | tf_op jit(solution)/shard_map/all_gather | solution.py:111
  111.1 4.9 %conditional.3 = (f32[2,2048]{1,0:T(2,128)}, f32[2,2048]{1,0:T(2,128)S(1)}) conditional(s32[]{:T(128)} %convert_element_type.72, () %tuple.34, (s32[2,8,64]{2,1,0:T(8,128)S(1)}, s32[256,8]{1,0:T(8,128)S(1)}, bf16[2,2048,128]{2,1,0:T(8,128)(2,1)S(1)}, bf16[512,2,128]{2,0,1:T(8,128)(2,1)S(1)}) %tuple.56), branch_computations={%region_2.3_spmd, %region_3.6_spmd} | conditional | flops 555741184 | bytes 18251792 | solution.py:101
  111.3 1.3 fusion
  112.7 0.6 broadcast_maximum_fusion
  113.3 2.7 %fusion.1 = f32[2,2048]{1,0:T(2,128)S(1)} fusion(f32[2,2048,512]{1,2,0:T(8,128)S(1)} %get-tuple-element.122, f32[2,2048]{1,0:T(2,128)} %broadcast_maximum_fusion, s32[2048]{0:T(1024)S(1)} %le.37, s32[2,512]{1,0:T(2,128)S(1)} %le.35), kind=kLoop, calls=%fused_computation.3 | loop fusion | flops 10481664 | bytes 8433664 | tf_op jit(solution)/shard_map/cond/branch_1_fun/reduce_sum | solution.py:98
  116.1 1.3 add.98
  117.4 3.5 %conditional.4 = (bf16[2,2048,128]{2,1,0:T(8,128)(2,1)S(1)}) conditional(s32[]{:T(128)} %convert_element_type.72, () %tuple.33, (s32[2,8,64]{2,1,0:T(8,128)S(1)}, s32[256,8]{1,0:T(8,128)S(1)}, bf16[512,2,256]{2,0,1:T(8,128)(2,1)S(1)}, bf16[2,2048,128]{2,1,0:T(8,128)(2,1)S(1)}, f32[2,2048]{1,0:T(2,128)}) %tuple.57), branch_computations={%region_6.7_spmd, %region_7.8_spmd} | conditional | flops 1084227584 | bytes 2674696 | solution.py:122
  117.6 3.3 %fusion.2 = bf16[2,2048,128]{2,1,0:T(8,128)(2,1)S(1)} fusion(bf16[2,2048,128]{2,1,0:T(8,128)(2,1)S(1)} %get-tuple-element.67, f32[2,2048]{1,0:T(2,128)} %get-tuple-element.69, s32[2,512]{1,0:T(2,128)S(1)} %le.50, s32[2048]{0:T(1024)S(1)} %le.52, bf16[512,2,256]{2,0,1:T(8,128)(2,1)S(1)} %get-tuple-element.68), kind=kOutput, calls=%fused_computation.6 | convolution fusion | flops 1084227584 | bytes 2650112 | tf_op jit(solution)/shard_map/cond/branch_1_fun/hrn,nhd->hrd/dot_general | solution.py:115
  121.1 21.8 %conditional.5 = (bf16[512,2,256]{0,2,1:T(8,128)(2,1)S(1)}) conditional(s32[]{:T(128)} %convert_element_type.72, () %tuple.37, (s32[2,8,64]{2,1,0:T(8,128)S(1)}, s32[256,8]{1,0:T(8,128)S(1)}, bf16[512,2,256]{2,0,1:T(8,128)(2,1)}, bf16[2,2048,128]{2,1,0:T(8,128)(2,1)}, f32[2,2048]{1,0:T(2,128)}, /*index=5*/bf16[2,4,64,8,128]{4,3,2,0,1:T(8,128)(2,1)}, ...), branch_computations={%region_8.9_spmd, %region_9.11_spmd} | conditional | flops 2175528960 | bytes 49414264 | solution.py:154
  121.3 0.7 le.55
  122.1 1.3 copy.62
  123.4 0.7 multiply_reduce_fusion
  124.1 0.3 copy-done.2
  124.4 5.9 %fusion.20 = f32[2,2048,512]{2,1,0:T(8,128)} fusion(bf16[2,2048,128]{2,1,0:T(8,128)(2,1)} %get-tuple-element.117, bf16[512,2,256]{2,0,1:T(8,128)(2,1)} %get-tuple-element.73), kind=kOutput, calls=%fused_computation.23 | convolution fusion | flops 536870912 | bytes 9699328 | tf_op jit(solution)/shard_map/cond/branch_1_fun/hrd,nhd->hrn/dot_general | solution.py:76
  130.3 7.0 %fusion.17 = bf16[512,2,128]{0,2,1:T(8,128)(2,1)S(1)} fusion(bf16[2,2048,128]{2,1,0:T(8,128)(2,1)S(1)} %copy-done.1, f32[2,2048,512]{2,1,0:T(8,128)} %fusion.20, bf16[2,2048,128]{2,1,0:T(8,128)(2,1)S(1)} %bitcast.57, f32[2,2048]{1,0:T(2,128)S(1)} %multiply_reduce_fusion, f32[2,2048]{1,0:T(2,128)} %get-tuple-element.74, s32[2,512]{1,0:T(2,128)S(1)} %copy-done.5, ...), kind=kOutput, calls=%fused_computation.20 | convolution fusion | flops 1088684032 | bytes 11055104 | tf_op jit(solution)/shard_map/cond/branch_1_fun/hrn,hrd->nhd/dot_general | solution.py:149
  137.2 5.6 %fusion.13 = bf16[512,2,128]{0,2,1:T(8,128)(2,1)S(1)} fusion(bf16[2,2048,128]{2,1,0:T(8,128)(2,1)S(1)} %bitcast.58, f32[2,2048,512]{2,1,0:T(8,128)} %fusion.20, f32[2,2048]{1,0:T(2,128)} %get-tuple-element.74, s32[2,512]{1,0:T(2,128)S(1)} %copy-done.5, s32[2048]{0:T(1024)S(1)} %le.57), kind=kOutput, calls=%fused_computation.18 | convolution fusion | flops 547356672 | bytes 9728000 | tf_op jit(solution)/shard_map/cond/branch_1_fun/hrn,hrd->nhd/dot_general | solution.py:138
  142.9 1.0 copy.63
  144.0 1.2 copy.58
  145.1 3.5 %all-to-all-start.3 = ((bf16[2,256,8,128]{3,2,0,1:T(8,128)(2,1)}), bf16[2,256,8,128]{3,2,0,1:T(8,128)(2,1)S(1)}, u32[]{:S(2)}, u32[]{:S(2)}) async-start(bf16[2,256,8,128]{3,2,0,1:T(8,128)(2,1)} %copy.58), calls=%async_computation.3 | async-start | bytes 2097152 | tf_op jit(solution)/shard_map/all_to_all | solution.py:124
  148.7 59.2 %reduce-scatter.2.cloned.1.call-done = bf16[64,2,256]{2,0,1:T(8,128)(2,1)} async-done(((bf16[512,2,256]{2,0,1:T(8,128)(2,1)}), bf16[64,2,256]{2,0,1:T(8,128)(2,1)}) %reduce-scatter.2.cloned.1.call-update) | async-done | bytes 65552 | tf_op jit(solution)/shard_map/reduce_scatter | solution.py:157
  207.9 0.7 slice.52
  208.6 3.4 %collective-permute-start.1 = (bf16[1,2,256]{2,0,1:T(2,128)(2,1)S(1)}, bf16[1,2,256]{2,0,1:T(2,128)(2,1)S(1)}, u32[]{:S(2)}, u32[]{:S(2)}) collective-permute-start(bf16[1,2,256]{2,0,1:T(2,128)(2,1)S(1)} %slice.52), channel_id=1, source_target_pairs={{0,4},{4,8},{8,12},{12,16},{16,20},{20,24},{24,28},{1,5},{5,9},{9,... | collective-permute-start | bytes 3080 | tf_op jit(solution)/shard_map/ppermute | solution.py:14
  212.1 2.9 %collective-permute-done.1 = bf16[1,2,256]{2,0,1:T(2,128)(2,1)S(1)} collective-permute-done((bf16[1,2,256]{2,0,1:T(2,128)(2,1)S(1)}, bf16[1,2,256]{2,0,1:T(2,128)(2,1)S(1)}, u32[]{:S(2)}, u32[]{:S(2)}) %collective-permute-start.1) | collective-permute-done | bytes 1056 | tf_op jit(solution)/shard_map/ppermute | solution.py:14
  215.0 1.1 fusion.26
  216.2 0.8 copy.66
  217.0 3.3 %all-to-all-start.6 = ((bf16[2,256,128]{2,0,1:T(2,128)(2,1)}), bf16[2,256,128]{2,0,1:T(2,128)(2,1)S(1)}, u32[]{:S(2)}, u32[]{:S(2)}) async-start(bf16[2,256,128]{2,0,1:T(2,128)(2,1)} %copy.66), calls=%async_computation.7 | async-start | bytes 262144 | tf_op jit(solution)/shard_map/all_to_all | solution.py:185
  220.3 1.2 copy.60
  221.5 0.8 copy.64
  222.3 2.6 %all-to-all-done.6 = bf16[2,256,128]{2,0,1:T(2,128)(2,1)S(1)} async-done(((bf16[2,256,128]{2,0,1:T(2,128)(2,1)}), bf16[2,256,128]{2,0,1:T(2,128)(2,1)S(1)}, u32[]{:S(2)}, u32[]{:S(2)}) %all-to-all-start.6) | async-done | bytes 131104 | tf_op jit(solution)/shard_map/all_to_all | solution.py:185
  224.9 3.3 %all-to-all-start.5 = ((bf16[2,256,128]{2,0,1:T(2,128)(2,1)}), bf16[2,256,128]{2,0,1:T(2,128)(2,1)S(1)}, u32[]{:S(2)}, u32[]{:S(2)}) async-start(bf16[2,256,128]{2,0,1:T(2,128)(2,1)} %copy.64), calls=%async_computation.6 | async-start | bytes 262144 | tf_op jit(solution)/shard_map/all_to_all | solution.py:178
  228.3 0.7 copy.67
  229.1 3.8 %all-to-all-done.5 = bf16[2,256,128]{2,0,1:T(2,128)(2,1)S(1)} async-done(((bf16[2,256,128]{2,0,1:T(2,128)(2,1)}), bf16[2,256,128]{2,0,1:T(2,128)(2,1)S(1)}, u32[]{:S(2)}, u32[]{:S(2)}) %all-to-all-start.5) | async-done | bytes 131104 | tf_op jit(solution)/shard_map/all_to_all | solution.py:178
  232.9 0.7 copy.65
  (46 shorter events, 2.0 us)
Async XLA Ops:
  7.2 7.9 %all-to-all-start = ((bf16[8,64,128]{2,1,0:T(8,128)(2,1)}), bf16[8,64,128]{2,1,0:T(8,128)(2,1)S(1)}, u32[]{:S(2)}, u32[]{:S(2)}) async-start(bf16[8,64,128]{2,1,0:T(8,128)(2,1)} %param.11), calls=%async_computation | async-start | bytes 262144 | tf_op jit(solution)/shard_map/all_to_all | solution.py:25
  15.1 7.9 %all-to-all-start.1 = ((bf16[8,64,128]{2,1,0:T(8,128)(2,1)}), bf16[8,64,128]{2,1,0:T(8,128)(2,1)S(1)}, u32[]{:S(2)}, u32[]{:S(2)}) async-start(bf16[8,64,128]{2,1,0:T(8,128)(2,1)} %param.12), calls=%async_computation.1 | async-start | bytes 262144 | tf_op jit(solution)/shard_map/all_to_all | solution.py:26
  23.0 18.0 %all-to-all-start.2 = ((bf16[8,64,8,128]{3,2,1,0:T(8,128)(2,1)}), bf16[8,64,8,128]{3,2,1,0:T(8,128)(2,1)S(1)}, u32[]{:S(2)}, u32[]{:S(2)}) async-start(bf16[8,64,8,128]{3,2,1,0:T(8,128)(2,1)} %param.13), calls=%async_computation.2 | async-start | bytes 2097152 | tf_op jit(solution)/shard_map/all_to_all | solution.py:27
  41.0 80.1 %all-to-all-start.4 = ((bf16[8,64,8,128]{3,2,1,0:T(8,128)(2,1)}), bf16[8,64,8,128]{3,2,1,0:T(8,128)(2,1)}, u32[]{:S(2)}, u32[]{:S(2)}) async-start(bf16[8,64,8,128]{3,2,1,0:T(8,128)(2,1)} %param.14), calls=%async_computation.4 | async-start | bytes 2097152 | tf_op jit(solution)/shard_map/all_to_all | solution.py:28
  45.3 162.7 %reduce-scatter.2.cloned.1.call-start = ((), (), s32[]{:S(2)}) async-start(), calls=%async_computation.8 | async-start | bytes 589824 | tf_op jit(solution)/shard_map/reduce_scatter | solution.py:157
  45.5 5.5 %collective-permute-start = (f32[1,2,256]{2,0,1:T(1,128)S(1)}, f32[1,2,256]{2,0,1:T(1,128)S(1)}, u32[]{:S(2)}, u32[]{:S(2)}) collective-permute-start(f32[1,2,256]{2,0,1:T(1,128)S(1)} %slice.50), channel_id=1, source_target_pairs={{4,0},{8,4},{12,8},{16,12},{20,16},{24,20},{28,24},{5,1},{9,5},{13... | collective-permute-start | bytes 6152 | tf_op jit(solution)/shard_map/ppermute | solution.py:14
  111.0 6.5 %copy-start.4 = (bf16[512,2,256]{2,0,1:T(8,128)(2,1)}, bf16[512,2,256]{2,0,1:T(8,128)(2,1)S(1)}, u32[]{:S(2)}) copy-start(bf16[512,2,256]{2,0,1:T(8,128)(2,1)S(1)} %all_gather.7) | copy-start | bytes 1572868
  111.0 6.4 %copy-start = (bf16[2,4,64,8,128]{4,3,2,1,0:T(8,128)(2,1)}, bf16[2,4,64,8,128]{4,3,2,1,0:T(8,128)(2,1)S(1)}, u32[]{:S(2)}) copy-start(bf16[2,4,64,8,128]{4,3,2,1,0:T(8,128)(2,1)S(1)} %copy.57) | copy-start | bytes 3145732
  122.1 8.2 %copy-start.5 = (s32[2,512]{1,0:T(2,128)S(1)}, s32[2,512]{1,0:T(2,128)}, u32[]{:S(2)}) copy-start(s32[2,512]{1,0:T(2,128)} %le.55) | copy-start | bytes 12292 | tf_op jit(solution)/shard_map/cond
  123.4 1.0 copy-start.2
  124.4 5.9 %copy-start.1 = (bf16[2,2048,128]{2,1,0:T(8,128)(2,1)S(1)}, bf16[2,2048,128]{2,1,0:T(8,128)(2,1)}, u32[]{:S(2)}) copy-start(bf16[2,2048,128]{2,1,0:T(8,128)(2,1)} %get-tuple-element.117) | copy-start | bytes 3145732 | tf_op jit(solution)/shard_map/cond
  124.4 5.9 %copy-start.3 = (bf16[2,4,64,8,128]{4,3,2,1,0:T(8,128)(2,1)S(1)}, bf16[2,4,64,8,128]{4,3,2,1,0:T(8,128)(2,1)}, u32[]{:S(2)}) copy-start(bf16[2,4,64,8,128]{4,3,2,1,0:T(8,128)(2,1)} %copy-done.2) | copy-start | bytes 3145732 | tf_op jit(solution)/shard_map/cond
  145.1 71.9 %all-to-all-start.3 = ((bf16[2,256,8,128]{3,2,0,1:T(8,128)(2,1)}), bf16[2,256,8,128]{3,2,0,1:T(8,128)(2,1)S(1)}, u32[]{:S(2)}, u32[]{:S(2)}) async-start(bf16[2,256,8,128]{3,2,0,1:T(8,128)(2,1)} %copy.58), calls=%async_computation.3 | async-start | bytes 2097152 | tf_op jit(solution)/shard_map/all_to_all | solution.py:124
  208.6 6.4 %collective-permute-start.1 = (bf16[1,2,256]{2,0,1:T(2,128)(2,1)S(1)}, bf16[1,2,256]{2,0,1:T(2,128)(2,1)S(1)}, u32[]{:S(2)}, u32[]{:S(2)}) collective-permute-start(bf16[1,2,256]{2,0,1:T(2,128)(2,1)S(1)} %slice.52), channel_id=1, source_target_pairs={{0,4},{4,8},{8,12},{12,16},{16,20},{20,24},{24,28},{1,5},{5,9},{9,... | collective-permute-start | bytes 3080 | tf_op jit(solution)/shard_map/ppermute | solution.py:14
  217.0 7.9 %all-to-all-start.6 = ((bf16[2,256,128]{2,0,1:T(2,128)(2,1)}), bf16[2,256,128]{2,0,1:T(2,128)(2,1)S(1)}, u32[]{:S(2)}, u32[]{:S(2)}) async-start(bf16[2,256,128]{2,0,1:T(2,128)(2,1)} %copy.66), calls=%async_computation.7 | async-start | bytes 262144 | tf_op jit(solution)/shard_map/all_to_all | solution.py:185
  224.9 7.9 %all-to-all-start.5 = ((bf16[2,256,128]{2,0,1:T(2,128)(2,1)}), bf16[2,256,128]{2,0,1:T(2,128)(2,1)S(1)}, u32[]{:S(2)}, u32[]{:S(2)}) async-start(bf16[2,256,128]{2,0,1:T(2,128)(2,1)} %copy.64), calls=%async_computation.6 | async-start | bytes 262144 | tf_op jit(solution)/shard_map/all_to_all | solution.py:178
Sparse Core Ops, SparseCore 0:
  144.1 63.8 reduce-scatter.1
where the time goes:
time: 242 us; the launch traced here: 241 us
  waiting for transfers between devices  90.6 us (37%)
  blocking collectives  59.9 us (25%)
  starting transfers between devices  31.3 us (13%)
  matrix products  24.4 us (10%)
  between operations  14.9 us (6%)
  local copies, waits for them, and re-layouts  11 us (5%)
  other arithmetic  8.1 us (3%)
    reduce_scatter x1, waiting for transfers between devices, per_device(): lax.psum_scatter(partials.astype(jnp.bfloat16), 'ctx', scatter_dimension=...  59.2 us
    all_gather x1, blocking collectives, per_device(): pair_block = lax.all_gather(slot_pairs, 'ctx', axis=0, tiled=True)  31.5 us
    all_gather x1, blocking collectives, per_device(): lax.all_gather(slot_pairs[:, :, :head_dim], 'ctx', axis=0, tiled=True)  28.4 us
    all_to_all x1, waiting for transfers between devices, per_device(): lax.all_to_all(queries, 'head', split_axis=0, concat_axis=1, tiled=True)  13.4 us
    dot_general x2, matrix products, block_scores(): jnp.einsum('hrd,nhd->hrn', query_rows, key_block, preferred_element_type=...  7.21 us
    dot_general x1, matrix products, grad_advance(): jnp.einsum('hrn,hrd->nhd', dscores, query_rows, preferred_element_type=jn...  6.96 us
    ppermute x2, starting transfers between devices, from_behind(): lax.ppermute(value, axis, [(source, source + steps) for source in range(i...  6.64 us
    dot_general x1, matrix products, grad_advance(): jnp.einsum('hrn,hrd->nhd', weights_low, grad_rows, preferred_element_type...  5.63 us
  transfers between devices with their start and end apart: 10, of which 8 were waited for; matrix products, arithmetic and copies ran while one was open for 8% of the time, Pallas kernels for 0%

commit v1 on v0

--- a/solution.py
+++ b/solution.py
@@ -8,6 +8,22 @@
 neg_big = -1e30
 
 
+def swapped_with_each(x, axis, split, join):
+    ways, here = (lax.axis_size(axis), lax.axis_index(axis))
+    width = x.shape[split] // ways
+    dims = list(x.shape)
+    dims[split] = width
+    height = dims[join]
+    dims[join] = height * ways
+    full = jnp.zeros(dims, x.dtype)
+    for mask in range(ways):
+        part = lax.dynamic_slice_in_dim(x, (here ^ mask) * width, width, axis=split)
+        if mask:
+            part = lax.ppermute(part, axis, [(d, d ^ mask) for d in range(ways)])
+        full = lax.dynamic_update_slice_in_dim(full, part, (here ^ mask) * height, axis=join)
+    return full
+
+
 def from_behind(value, axis, steps):
     count = lax.axis_size(axis)
     initial, last = (max(0, -steps), min(count, count - steps))
@@ -23,7 +39,7 @@
 def per_device(token_keys, token_values, queries, out_grad, slot_ids):
     keys_here, values_here, query_here, grad_here = (
         lax.all_to_all(token_keys, "head", split_axis=0, concat_axis=1, tiled=True),
-        lax.all_to_all(token_values, "head", split_axis=0, concat_axis=1, tiled=True),
+        swapped_with_each(token_values, "head", 0, 1),
         lax.all_to_all(queries, "head", split_axis=0, concat_axis=1, tiled=True),
         lax.all_to_all(out_grad, "head", split_axis=0, concat_axis=1, tiled=True),
     )

time: 242 us -> 235 us (0.971)
  waiting for transfers between devices: 90.6 us -> 83.6 us
    all_to_all x1 -> x0, waiting for transfers between devices: 4.58 us -> none  [per_device(): lax.all_to_all(token_values, 'head', split_axis=0, concat_axis=1, tiled=T...]
    all_to_all x1 -> x0, starting transfers between devices: 3.33 us -> none  [per_device(): lax.all_to_all(token_values, 'head', split_axis=0, concat_axis=1, tiled=T...]
    all_to_all x1, waiting for transfers between devices: 2.63 us -> 0.01 us  [per_device(): lax.all_to_all(token_keys, 'head', split_axis=0, concat_axis=1, tiled=True)]
  transfers between devices with their start and end apart: 10 -> 12, of which waited for: 8 -> 6; matrix products, arithmetic and copies ran while one was open for 8% -> 9% of each run, Pallas kernels for 0% -> 0%
where the time goes in v1:
time: 235 us; the launch traced here: 233 us
  waiting for transfers between devices  83.6 us (36%)
  blocking collectives  59.9 us (25%)
  starting transfers between devices  30.3 us (13%)
  matrix products  24.5 us (10%)
  between operations  14.9 us (6%)
  local copies, waits for them, and re-layouts  11.9 us (5%)
  other arithmetic  8.11 us (3%)
    reduce_scatter x1, waiting for transfers between devices, per_device(): lax.psum_scatter(partials.astype(jnp.bfloat16), 'ctx', scatter_dimension=...  59.2 us
    all_gather x1, blocking collectives, per_device(): pair_block = lax.all_gather(slot_pairs, 'ctx', axis=0, tiled=True)  31.5 us
    all_gather x1, blocking collectives, per_device(): lax.all_gather(slot_pairs[:, :, :head_dim], 'ctx', axis=0, tiled=True)  28.4 us
    all_to_all x1, waiting for transfers between devices, per_device(): lax.all_to_all(queries, 'head', split_axis=0, concat_axis=1, tiled=True)  13.6 us
    dot_general x2, matrix products, block_scores(): jnp.einsum('hrd,nhd->hrn', query_rows, key_block, preferred_element_type=...  7.24 us
    dot_general x1, matrix products, grad_advance(): jnp.einsum('hrn,hrd->nhd', dscores, query_rows, preferred_element_type=jn...  6.96 us
    ppermute x2, starting transfers between devices, from_behind(): lax.ppermute(value, axis, [(source, source + steps) for source in range(i...  6.65 us
    dot_general x1, matrix products, grad_advance(): jnp.einsum('hrn,hrd->nhd', weights_low, grad_rows, preferred_element_type...  5.63 us
  transfers between devices with their start and end apart: 12, of which 6 were waited for; matrix products, arithmetic and copies ran while one was open for 9% of the time, Pallas kernels for 0%

profile of v1, /device:TPU:8, one launch (start us, length us, event | category | flops | bytes accessed | tf_op | source)
XLA Modules:
  0.0 233.4 jit_solution(11360850656277990461)
XLA Ops:
  7.2 3.3 %all-to-all-start = ((bf16[8,64,128]{2,1,0:T(8,128)(2,1)}), bf16[8,64,128]{2,1,0:T(8,128)(2,1)S(1)}, u32[]{:S(2)}, u32[]{:S(2)}) async-start(bf16[8,64,128]{2,1,0:T(8,128)(2,1)} %param.11), calls=%async_computation | async-start | bytes 262144 | tf_op jit(solution)/shard_map/all_to_all | solution.py:41
  10.6 0.8 constant_dynamic-slice_fusion.2
  11.4 1.8 collective-permute-start.2
  13.2 0.4 collective-permute-start
  13.9 0.7 copy.68
  14.6 0.5 convert_reduce_fusion
  15.3 0.6 slice_reduce_fusion
  15.9 3.5 %all-to-all-start.1 = ((bf16[8,64,8,128]{3,2,1,0:T(8,128)(2,1)}), bf16[8,64,8,128]{3,2,1,0:T(8,128)(2,1)S(1)}, u32[]{:S(2)}, u32[]{:S(2)}) async-start(bf16[8,64,8,128]{3,2,1,0:T(8,128)(2,1)} %param.13), calls=%async_computation.1 | async-start | bytes 2097152 | tf_op jit(solution)/shard_map/all_to_all | solution.py:43
  19.4 0.7 fusion.38
  20.3 13.6 %all-to-all-done.1 = bf16[8,64,8,128]{3,2,1,0:T(8,128)(2,1)S(1)} async-done(((bf16[8,64,8,128]{3,2,1,0:T(8,128)(2,1)}), bf16[8,64,8,128]{3,2,1,0:T(8,128)(2,1)S(1)}, u32[]{:S(2)}, u32[]{:S(2)}) %all-to-all-start.1) | async-done | bytes 1048608 | tf_op jit(solution)/shard_map/all_to_all | solution.py:43
  33.9 4.3 %all-to-all-start.3 = ((bf16[8,64,8,128]{3,2,1,0:T(8,128)(2,1)}), bf16[8,64,8,128]{3,2,1,0:T(8,128)(2,1)}, u32[]{:S(2)}, u32[]{:S(2)}) async-start(bf16[8,64,8,128]{3,2,1,0:T(8,128)(2,1)} %param.14), calls=%async_computation.3 | async-start | bytes 2097152 | tf_op jit(solution)/shard_map/all_to_all | solution.py:44
  38.2 0.2 convolution_bitcast_fusion
  38.4 3.3 %collective-permute-start.3 = (f32[1,2,256]{2,0,1:T(1,128)S(1)}, f32[1,2,256]{2,0,1:T(1,128)S(1)}, u32[]{:S(2)}, u32[]{:S(2)}) collective-permute-start(f32[1,2,256]{2,0,1:T(1,128)S(1)} %slice.50), channel_id=1, source_target_pairs={{4,0},{8,4},{12,8},{16,12},{20,16},{24,20},{28,24},{5,1},{9,5},{13... | collective-permute-start | bytes 6152 | tf_op jit(solution)/shard_map/ppermute | solution.py:30
  42.4 1.5 collective-permute-done.3
  44.0 28.4 %all_gather.8 = bf16[512,2,128]{2,0,1:T(8,128)(2,1)S(1)} all-gather(bf16[64,2,128]{2,0,1:T(8,128)(2,1)S(1)} %slice.51), channel_id=1, replica_groups=mesh['ctx'=8,'head'=4] {'ctx'}, dimensions={0}, use_global_device_ids=true | all-gather | bytes 294912 | tf_op jit(solution)/shard_map/all_gather | solution.py:108
  72.3 31.5 %all_gather.7 = bf16[512,2,256]{2,0,1:T(8,128)(2,1)S(1)} all-gather(bf16[64,2,256]{2,0,1:T(8,128)(2,1)S(1)} %fusion.31), channel_id=1, replica_groups=mesh['ctx'=8,'head'=4] {'ctx'}, dimensions={0}, use_global_device_ids=true | all-gather | bytes 589824 | tf_op jit(solution)/shard_map/all_gather | solution.py:127
  104.0 5.0 %conditional.3 = (f32[2,2048]{1,0:T(2,128)}, f32[2,2048]{1,0:T(2,128)S(1)}) conditional(s32[]{:T(128)} %convert_element_type.72, () %tuple.34, (s32[2,8,64]{2,1,0:T(8,128)S(1)}, s32[256,8]{1,0:T(8,128)S(1)}, bf16[2,2048,128]{2,1,0:T(8,128)(2,1)S(1)}, bf16[512,2,128]{2,0,1:T(8,128)(2,1)S(1)}) %tuple.59), branch_computations={%region_2.3_spmd, %region_3.6_spmd} | conditional | flops 555741184 | bytes 18251792 | solution.py:117
  104.2 1.3 fusion
  105.6 0.6 broadcast_maximum_fusion
  106.2 2.7 %fusion.1 = f32[2,2048]{1,0:T(2,128)S(1)} fusion(f32[2,2048,512]{1,2,0:T(8,128)S(1)} %get-tuple-element.122, f32[2,2048]{1,0:T(2,128)} %broadcast_maximum_fusion, s32[2048]{0:T(1024)S(1)} %le.37, s32[2,512]{1,0:T(2,128)S(1)} %le.35), kind=kLoop, calls=%fused_computation.3 | loop fusion | flops 10481664 | bytes 8433664 | tf_op jit(solution)/shard_map/cond/branch_1_fun/reduce_sum | solution.py:114
  109.0 1.3 add.130
  110.3 3.5 %conditional.4 = (bf16[2,2048,128]{2,1,0:T(8,128)(2,1)S(1)}) conditional(s32[]{:T(128)} %convert_element_type.72, () %tuple.33, (s32[2,8,64]{2,1,0:T(8,128)S(1)}, s32[256,8]{1,0:T(8,128)S(1)}, bf16[512,2,256]{2,0,1:T(8,128)(2,1)S(1)}, bf16[2,2048,128]{2,1,0:T(8,128)(2,1)S(1)}, f32[2,2048]{1,0:T(2,128)}) %tuple.60), branch_computations={%region_6.7_spmd, %region_7.8_spmd} | conditional | flops 1084227584 | bytes 2674696 | solution.py:138
  110.5 3.3 %fusion.2 = bf16[2,2048,128]{2,1,0:T(8,128)(2,1)S(1)} fusion(bf16[2,2048,128]{2,1,0:T(8,128)(2,1)S(1)} %get-tuple-element.67, f32[2,2048]{1,0:T(2,128)} %get-tuple-element.69, s32[2,512]{1,0:T(2,128)S(1)} %le.50, s32[2048]{0:T(1024)S(1)} %le.52, bf16[512,2,256]{2,0,1:T(8,128)(2,1)S(1)} %get-tuple-element.68), kind=kOutput, calls=%fused_computation.6 | convolution fusion | flops 1084227584 | bytes 2650112 | tf_op jit(solution)/shard_map/cond/branch_1_fun/hrn,nhd->hrd/dot_general | solution.py:131
  114.0 21.8 %conditional.5 = (bf16[512,2,256]{0,2,1:T(8,128)(2,1)S(1)}) conditional(s32[]{:T(128)} %convert_element_type.72, () %tuple.37, (s32[2,8,64]{2,1,0:T(8,128)S(1)}, s32[256,8]{1,0:T(8,128)S(1)}, bf16[512,2,256]{2,0,1:T(8,128)(2,1)}, bf16[2,2048,128]{2,1,0:T(8,128)(2,1)}, f32[2,2048]{1,0:T(2,128)}, /*index=5*/bf16[2,4,64,8,128]{4,3,2,0,1:T(8,128)(2,1)}, ...), branch_computations={%region_8.9_spmd, %region_9.11_spmd} | conditional | flops 2175528960 | bytes 49414264 | solution.py:170
  114.2 0.7 le.55
  115.0 1.3 copy.57
  116.3 0.7 multiply_reduce_fusion
  117.0 0.3 copy-done.2
  117.2 5.9 %fusion.20 = f32[2,2048,512]{2,1,0:T(8,128)} fusion(bf16[2,2048,128]{2,1,0:T(8,128)(2,1)} %get-tuple-element.117, bf16[512,2,256]{2,0,1:T(8,128)(2,1)} %get-tuple-element.73), kind=kOutput, calls=%fused_computation.23 | convolution fusion | flops 536870912 | bytes 9699328 | tf_op jit(solution)/shard_map/cond/branch_1_fun/hrd,nhd->hrn/dot_general | solution.py:92
  123.1 7.0 %fusion.17 = bf16[512,2,128]{0,2,1:T(8,128)(2,1)S(1)} fusion(bf16[2,2048,128]{2,1,0:T(8,128)(2,1)S(1)} %copy-done.1, f32[2,2048,512]{2,1,0:T(8,128)} %fusion.20, bf16[2,2048,128]{2,1,0:T(8,128)(2,1)S(1)} %bitcast.53, f32[2,2048]{1,0:T(2,128)S(1)} %multiply_reduce_fusion, f32[2,2048]{1,0:T(2,128)} %get-tuple-element.74, s32[2,512]{1,0:T(2,128)S(1)} %copy-done.5, ...), kind=kOutput, calls=%fused_computation.20 | convolution fusion | flops 1088684032 | bytes 11055104 | tf_op jit(solution)/shard_map/cond/branch_1_fun/hrn,hrd->nhd/dot_general | solution.py:165
  130.1 5.6 %fusion.13 = bf16[512,2,128]{0,2,1:T(8,128)(2,1)S(1)} fusion(bf16[2,2048,128]{2,1,0:T(8,128)(2,1)S(1)} %bitcast.54, f32[2,2048,512]{2,1,0:T(8,128)} %fusion.20, f32[2,2048]{1,0:T(2,128)} %get-tuple-element.74, s32[2,512]{1,0:T(2,128)S(1)} %copy-done.5, s32[2048]{0:T(1024)S(1)} %le.57), kind=kOutput, calls=%fused_computation.18 | convolution fusion | flops 547356672 | bytes 9728000 | tf_op jit(solution)/shard_map/cond/branch_1_fun/hrn,hrd->nhd/dot_general | solution.py:154
  135.8 1.0 copy.58
  136.8 1.2 copy.53
  138.0 3.5 %all-to-all-start.2 = ((bf16[2,256,8,128]{3,2,0,1:T(8,128)(2,1)}), bf16[2,256,8,128]{3,2,0,1:T(8,128)(2,1)S(1)}, u32[]{:S(2)}, u32[]{:S(2)}) async-start(bf16[2,256,8,128]{3,2,0,1:T(8,128)(2,1)} %copy.53), calls=%async_computation.2 | async-start | bytes 2097152 | tf_op jit(solution)/shard_map/all_to_all | solution.py:140
  141.6 59.2 %reduce-scatter.2.cloned.1.call-done = bf16[64,2,256]{2,0,1:T(8,128)(2,1)} async-done(((bf16[512,2,256]{2,0,1:T(8,128)(2,1)}), bf16[64,2,256]{2,0,1:T(8,128)(2,1)}) %reduce-scatter.2.cloned.1.call-update) | async-done | bytes 65552 | tf_op jit(solution)/shard_map/reduce_scatter | solution.py:173
  200.8 0.7 slice.52
  201.5 3.4 %collective-permute-start.4 = (bf16[1,2,256]{2,0,1:T(2,128)(2,1)S(1)}, bf16[1,2,256]{2,0,1:T(2,128)(2,1)S(1)}, u32[]{:S(2)}, u32[]{:S(2)}) collective-permute-start(bf16[1,2,256]{2,0,1:T(2,128)(2,1)S(1)} %slice.52), channel_id=1, source_target_pairs={{0,4},{4,8},{8,12},{12,16},{16,20},{20,24},{24,28},{1,5},{5,9},{9,... | collective-permute-start | bytes 3080 | tf_op jit(solution)/shard_map/ppermute | solution.py:30
  205.0 2.9 %collective-permute-done.4 = bf16[1,2,256]{2,0,1:T(2,128)(2,1)S(1)} collective-permute-done((bf16[1,2,256]{2,0,1:T(2,128)(2,1)S(1)}, bf16[1,2,256]{2,0,1:T(2,128)(2,1)S(1)}, u32[]{:S(2)}, u32[]{:S(2)}) %collective-permute-start.4) | collective-permute-done | bytes 1056 | tf_op jit(solution)/shard_map/ppermute | solution.py:30
  207.8 1.1 fusion.26
  209.0 0.8 copy.61
  209.8 3.3 %all-to-all-start.5 = ((bf16[2,256,128]{2,0,1:T(2,128)(2,1)}), bf16[2,256,128]{2,0,1:T(2,128)(2,1)S(1)}, u32[]{:S(2)}, u32[]{:S(2)}) async-start(bf16[2,256,128]{2,0,1:T(2,128)(2,1)} %copy.61), calls=%async_computation.6 | async-start | bytes 262144 | tf_op jit(solution)/shard_map/all_to_all | solution.py:201
  213.2 1.2 copy.55
  214.3 0.8 copy.59
  215.1 2.6 %all-to-all-done.5 = bf16[2,256,128]{2,0,1:T(2,128)(2,1)S(1)} async-done(((bf16[2,256,128]{2,0,1:T(2,128)(2,1)}), bf16[2,256,128]{2,0,1:T(2,128)(2,1)S(1)}, u32[]{:S(2)}, u32[]{:S(2)}) %all-to-all-start.5) | async-done | bytes 131104 | tf_op jit(solution)/shard_map/all_to_all | solution.py:201
  217.8 3.3 %all-to-all-start.4 = ((bf16[2,256,128]{2,0,1:T(2,128)(2,1)}), bf16[2,256,128]{2,0,1:T(2,128)(2,1)S(1)}, u32[]{:S(2)}, u32[]{:S(2)}) async-start(bf16[2,256,128]{2,0,1:T(2,128)(2,1)} %copy.59), calls=%async_computation.5 | async-start | bytes 262144 | tf_op jit(solution)/shard_map/all_to_all | solution.py:194
  221.2 0.7 copy.62
  221.9 3.8 %all-to-all-done.4 = bf16[2,256,128]{2,0,1:T(2,128)(2,1)S(1)} async-done(((bf16[2,256,128]{2,0,1:T(2,128)(2,1)}), bf16[2,256,128]{2,0,1:T(2,128)(2,1)S(1)}, u32[]{:S(2)}, u32[]{:S(2)}) %all-to-all-start.4) | async-done | bytes 131104 | tf_op jit(solution)/shard_map/all_to_all | solution.py:194
  225.8 0.7 copy.60
  (54 shorter events, 2.2 us)
Async XLA Ops:
  7.2 8.7 %all-to-all-start = ((bf16[8,64,128]{2,1,0:T(8,128)(2,1)}), bf16[8,64,128]{2,1,0:T(8,128)(2,1)S(1)}, u32[]{:S(2)}, u32[]{:S(2)}) async-start(bf16[8,64,128]{2,1,0:T(8,128)(2,1)} %param.11), calls=%async_computation | async-start | bytes 262144 | tf_op jit(solution)/shard_map/all_to_all | solution.py:41
  11.4 8.8 %collective-permute-start.2 = (bf16[2,64,128]{2,1,0:T(8,128)(2,1)S(1)}, bf16[2,64,128]{2,1,0:T(8,128)(2,1)S(1)}, u32[]{:S(2)}, u32[]{:S(2)}) collective-permute-start(bf16[2,64,128]{2,1,0:T(8,128)(2,1)S(1)} %get-tuple-element.125), channel_id=1, source_target_pairs={{0,3},{1,2},{2,1},{3,0},{4,7},{5,6},{6,5},{7,4},{8,11},{9,10},{10,... | collective-permute-start | bytes 98312 | tf_op jit(solution)/shard_map/ppermute | solution.py:22
  13.2 7.0 %collective-permute-start = (bf16[2,64,128]{2,1,0:T(8,128)(2,1)S(1)}, bf16[2,64,128]{2,1,0:T(8,128)(2,1)S(1)}, u32[]{:S(2)}, u32[]{:S(2)}) collective-permute-start(bf16[2,64,128]{2,1,0:T(8,128)(2,1)S(1)} %get-tuple-element.126), channel_id=1, source_target_pairs={{0,1},{1,0},{2,3},{3,2},{4,5},{5,4},{6,7},{7,6},{8,9},{9,8},{10,11... | collective-permute-start | bytes 98312 | tf_op jit(solution)/shard_map/ppermute | solution.py:22
  13.5 6.7 %collective-permute-start.1 = (bf16[2,64,128]{2,1,0:T(8,128)(2,1)S(1)}, bf16[2,64,128]{2,1,0:T(8,128)(2,1)S(1)}, u32[]{:S(2)}, u32[]{:S(2)}) collective-permute-start(bf16[2,64,128]{2,1,0:T(8,128)(2,1)S(1)} %get-tuple-element.128), channel_id=1, source_target_pairs={{0,2},{1,3},{2,0},{3,1},{4,6},{5,7},{6,4},{7,5},{8,10},{9,11},{10,... | collective-permute-start | bytes 98312 | tf_op jit(solution)/shard_map/ppermute | solution.py:22
  15.9 18.0 %all-to-all-start.1 = ((bf16[8,64,8,128]{3,2,1,0:T(8,128)(2,1)}), bf16[8,64,8,128]{3,2,1,0:T(8,128)(2,1)S(1)}, u32[]{:S(2)}, u32[]{:S(2)}) async-start(bf16[8,64,8,128]{3,2,1,0:T(8,128)(2,1)} %param.13), calls=%async_computation.1 | async-start | bytes 2097152 | tf_op jit(solution)/shard_map/all_to_all | solution.py:43
  33.9 80.1 %all-to-all-start.3 = ((bf16[8,64,8,128]{3,2,1,0:T(8,128)(2,1)}), bf16[8,64,8,128]{3,2,1,0:T(8,128)(2,1)}, u32[]{:S(2)}, u32[]{:S(2)}) async-start(bf16[8,64,8,128]{3,2,1,0:T(8,128)(2,1)} %param.14), calls=%async_computation.3 | async-start | bytes 2097152 | tf_op jit(solution)/shard_map/all_to_all | solution.py:44
  38.1 162.6 %reduce-scatter.2.cloned.1.call-start = ((), (), s32[]{:S(2)}) async-start(), calls=%async_computation.7 | async-start | bytes 589824 | tf_op jit(solution)/shard_map/reduce_scatter | solution.py:173
  38.4 5.5 %collective-permute-start.3 = (f32[1,2,256]{2,0,1:T(1,128)S(1)}, f32[1,2,256]{2,0,1:T(1,128)S(1)}, u32[]{:S(2)}, u32[]{:S(2)}) collective-permute-start(f32[1,2,256]{2,0,1:T(1,128)S(1)} %slice.50), channel_id=1, source_target_pairs={{4,0},{8,4},{12,8},{16,12},{20,16},{24,20},{28,24},{5,1},{9,5},{13... | collective-permute-start | bytes 6152 | tf_op jit(solution)/shard_map/ppermute | solution.py:30
  103.8 6.5 %copy-start.4 = (bf16[512,2,256]{2,0,1:T(8,128)(2,1)}, bf16[512,2,256]{2,0,1:T(8,128)(2,1)S(1)}, u32[]{:S(2)}) copy-start(bf16[512,2,256]{2,0,1:T(8,128)(2,1)S(1)} %all_gather.7) | copy-start | bytes 1572868
  103.9 6.4 %copy-start = (bf16[2,4,64,8,128]{4,3,2,1,0:T(8,128)(2,1)}, bf16[2,4,64,8,128]{4,3,2,1,0:T(8,128)(2,1)S(1)}, u32[]{:S(2)}) copy-start(bf16[2,4,64,8,128]{4,3,2,1,0:T(8,128)(2,1)S(1)} %copy.52) | copy-start | bytes 3145732
  115.0 8.2 %copy-start.5 = (s32[2,512]{1,0:T(2,128)S(1)}, s32[2,512]{1,0:T(2,128)}, u32[]{:S(2)}) copy-start(s32[2,512]{1,0:T(2,128)} %le.55) | copy-start | bytes 12292 | tf_op jit(solution)/shard_map/cond
  116.3 1.0 copy-start.2
  117.2 5.9 %copy-start.1 = (bf16[2,2048,128]{2,1,0:T(8,128)(2,1)S(1)}, bf16[2,2048,128]{2,1,0:T(8,128)(2,1)}, u32[]{:S(2)}) copy-start(bf16[2,2048,128]{2,1,0:T(8,128)(2,1)} %get-tuple-element.117) | copy-start | bytes 3145732 | tf_op jit(solution)/shard_map/cond
  117.2 5.9 %copy-start.3 = (bf16[2,4,64,8,128]{4,3,2,1,0:T(8,128)(2,1)S(1)}, bf16[2,4,64,8,128]{4,3,2,1,0:T(8,128)(2,1)}, u32[]{:S(2)}) copy-start(bf16[2,4,64,8,128]{4,3,2,1,0:T(8,128)(2,1)} %copy-done.2) | copy-start | bytes 3145732 | tf_op jit(solution)/shard_map/cond
  138.0 71.8 %all-to-all-start.2 = ((bf16[2,256,8,128]{3,2,0,1:T(8,128)(2,1)}), bf16[2,256,8,128]{3,2,0,1:T(8,128)(2,1)S(1)}, u32[]{:S(2)}, u32[]{:S(2)}) async-start(bf16[2,256,8,128]{3,2,0,1:T(8,128)(2,1)} %copy.53), calls=%async_computation.2 | async-start | bytes 2097152 | tf_op jit(solution)/shard_map/all_to_all | solution.py:140
  201.5 6.4 %collective-permute-start.4 = (bf16[1,2,256]{2,0,1:T(2,128)(2,1)S(1)}, bf16[1,2,256]{2,0,1:T(2,128)(2,1)S(1)}, u32[]{:S(2)}, u32[]{:S(2)}) collective-permute-start(bf16[1,2,256]{2,0,1:T(2,128)(2,1)S(1)} %slice.52), channel_id=1, source_target_pairs={{0,4},{4,8},{8,12},{12,16},{16,20},{20,24},{24,28},{1,5},{5,9},{9,... | collective-permute-start | bytes 3080 | tf_op jit(solution)/shard_map/ppermute | solution.py:30
  209.8 7.9 %all-to-all-start.5 = ((bf16[2,256,128]{2,0,1:T(2,128)(2,1)}), bf16[2,256,128]{2,0,1:T(2,128)(2,1)S(1)}, u32[]{:S(2)}, u32[]{:S(2)}) async-start(bf16[2,256,128]{2,0,1:T(2,128)(2,1)} %copy.61), calls=%async_computation.6 | async-start | bytes 262144 | tf_op jit(solution)/shard_map/all_to_all | solution.py:201
  217.8 7.9 %all-to-all-start.4 = ((bf16[2,256,128]{2,0,1:T(2,128)(2,1)}), bf16[2,256,128]{2,0,1:T(2,128)(2,1)S(1)}, u32[]{:S(2)}, u32[]{:S(2)}) async-start(bf16[2,256,128]{2,0,1:T(2,128)(2,1)} %copy.59), calls=%async_computation.5 | async-start | bytes 262144 | tf_op jit(solution)/shard_map/all_to_all | solution.py:194
Sparse Core Ops, SparseCore 0:
  136.9 63.7 reduce-scatter.1
